TPU v7x, 32 devices: a whole 2x2x4 slice. The times are simulated.
32 devices in a mesh: groups: 2 (over x), shot: 16 (over z, y, core).
Axes of the slice: x: 2, y: 2, z: 4, core: 2. Of those that a mesh axis runs over, the one named last changes fastest.
Arguments:
- courant_sq: float32 [128, 32, 128], P('groups'), parts along dimension 0, may hold values from 0.05 to 0.2
- wave_now: float32 [512, 32, 128], P(('groups', 'shot')), parts along dimension 0, may hold values from -6 to 6
- wave_before: float32 [512, 32, 128], P(('groups', 'shot')), parts along dimension 0, may hold values from -6 to 6
- wavelet: float32 [32, 8], P(('groups', 'shot')), parts along dimension 0, may hold values from -24 to 24
- source_cell: int32 [32], P(('groups', 'shot')), parts along dimension 0, may hold values from 0 to 65535, as said below
- receiver_cell: int32 [8192], P(('groups', 'shot')), parts along dimension 0, may hold values from 0 to 65535, as said below
- send_order: int32 [8192], P(('groups', 'shot')), parts along dimension 0, may hold values from 0 to 255, as said below
- observed: float32 [512, 128], P(('groups', 'shot')), parts along dimension 0, may hold values from -6 to 6
Outputs:
- gradient_slabs: float32 [128, 32, 128], P(('groups', 'shot')), parts along dimension 0
There are 2 independent parts, one for each index of `groups`. A program takes and returns all parts, laid end to end along the dimension named above; each array names one. Nothing has to cross between parts.
Inputs may be any that keep to these rules, and one draw needn't show every extreme that they name: `source_cell`: a local cell index (x * 32 + y) * 128 + z of a block of 16 planes. `receiver_cell`: a local cell index (x * 32 + y) * 128 + z of a block of 16 planes. `send_order`: each aligned block of 256 entries is a permutation of 0 to 255.
All inputs are finite; a program needn't handle non-finite values.
Results may differ from a plain program's by a relative error of at most 0.00021.
Values sent between devices are 32-bit elements; how exact they have to be, the bound alone decides.
A program may use at most 64 MiB of HBM per device.

v0:
```python
import jax
import jax.numpy as jnp
from jax import lax
from jax.sharding import PartitionSpec as P

NT = 8
PIECES = 4


stencil_center = -205.0 / 72.0
stencil_weights = (8.0 / 5.0, -1.0 / 5.0, 8.0 / 315.0, -1.0 / 560.0)


def extended_2(cells, sides, width):
    for axis, dim in sides:
        count = lax.axis_size(axis)
        head = lax.slice_in_dim(cells, 0, width, axis=dim)
        tail = lax.slice_in_dim(cells, cells.shape[dim] - width, cells.shape[dim], axis=dim)
        cells = jnp.concatenate(
            [
                lax.ppermute(tail, axis, [(i, (i + 1) % count) for i in range(count)]),
                cells,
                lax.ppermute(head, axis, [((i + 1) % count, i) for i in range(count)]),
            ],
            axis=dim,
        )
    return cells


def shifted_2(value, axis, steps):
    count = lax.axis_size(axis)
    pairs = [(source, (source + steps) % count) for source in range(count)]
    return lax.ppermute(value, axis, pairs)


def shifted(values, offset, axis_pos):
    length = values.shape[axis_pos]
    filler_shape = list(values.shape)
    filler_shape[axis_pos] = abs(offset)
    filler = jnp.zeros(filler_shape, values.dtype)
    if offset > 0:
        return jnp.concatenate(
            [lax.slice_in_dim(values, offset, length, axis=axis_pos), filler], axis_pos
        )
    return jnp.concatenate(
        [filler, lax.slice_in_dim(values, 0, length + offset, axis=axis_pos)], axis_pos
    )


def laplace_rows(extended, start, count_rows):
    center = lax.slice_in_dim(extended, start, start + count_rows, axis=0)
    summed = 3.0 * stencil_center * center
    for distance in range(1, len(stencil_weights) + 1):
        weight = stencil_weights[distance - 1]
        beside_all = lax.slice_in_dim(
            extended, start + distance, start + distance + count_rows, axis=0
        )
        beside_all = beside_all + lax.slice_in_dim(
            extended, start - distance, start - distance + count_rows, axis=0
        )
        beside_all = beside_all + shifted(center, distance, 1) + shifted(center, -distance, 1)
        beside_all = beside_all + shifted(center, distance, 2) + shifted(center, -distance, 2)
        summed = summed + weight * beside_all
    return summed


def cell_tables(cells, rows_total, depth):
    row_of = cells // depth
    col_of = cells % depth
    row_table = (row_of[:, None] == jnp.arange(rows_total, dtype=jnp.int32)[None, :]).astype(
        jnp.float32
    )
    col_table = (col_of[:, None] == jnp.arange(depth, dtype=jnp.int32)[None, :]).astype(jnp.float32)
    return (row_table, col_table)


def inject(wavefield, tables, amounts):
    row_table, col_table = tables
    weighted = row_table * amounts[:, None]
    added = lax.dot_general(
        weighted,
        col_table,
        (((0,), (0,)), ((), ())),
        precision=lax.Precision.HIGHEST,
        preferred_element_type=jnp.float32,
    )
    return wavefield + added.reshape(wavefield.shape)


def extract(wavefield, tables):
    row_table, col_table = tables
    flat_rows = wavefield.reshape(row_table.shape[1], col_table.shape[1])
    picked = jnp.dot(
        row_table, flat_rows, precision=lax.Precision.HIGHEST, preferred_element_type=jnp.float32
    )
    return jnp.sum(picked * col_table, axis=1)


def per_device(
    courant_sq, wave_now, wave_before, wavelet, source_cell, receiver_cell, send_order, observed
):
    device_count = lax.axis_size("shot")
    device_index = lax.axis_index("shot")
    domain_piece = device_index % PIECES
    piece_rows, span_y, span_z = wave_now.shape
    stencil_reach = len(stencil_weights)
    courant_piece = lax.dynamic_slice_in_dim(courant_sq, domain_piece * piece_rows, piece_rows, 0)
    plane_rows = piece_rows * span_y
    source_tables = cell_tables(source_cell, plane_rows, span_z)
    ordered_cells = receiver_cell[send_order]
    receiver_tables = cell_tables(ordered_cells, plane_rows, span_z)

    def single_step(current, previous, tables, amounts):
        extended = extended_2(current, (("shot", 0),), stencil_reach)
        updated = (
            2.0 * current
            - previous
            + courant_piece * laplace_rows(extended, stencil_reach, piece_rows)
        )
        return inject(updated, tables, amounts)

    def advance_all(current, previous, injections):
        produced = []
        for tables, amounts in injections:
            updated = single_step(current, previous, tables, amounts)
            produced.append(updated)
            previous, current = (current, updated)
        return produced

    forward_list = advance_all(
        wave_now,
        wave_before,
        [(source_tables, wavelet[0, step_index : step_index + 1]) for step_index in range(NT)],
    )
    traces = jnp.stack([extract(wavefield, receiver_tables) for wavefield in forward_list])
    receiver_count = receiver_cell.shape[0]
    per_owner = receiver_count // device_count
    packed = (
        traces.reshape(NT, device_count, per_owner)
        .transpose(1, 0, 2)
        .reshape(device_count, NT * per_owner)
    )
    arrived = lax.all_to_all(packed, "shot", split_axis=0, concat_axis=0, tiled=True)
    returned = lax.all_to_all(arrived - observed, "shot", split_axis=0, concat_axis=0, tiled=True)
    misfit = (
        returned.reshape(device_count, NT, per_owner).transpose(1, 0, 2).reshape(NT, receiver_count)
    )
    empty_field = jnp.zeros_like(wave_now)
    adjoint_now = inject(empty_field, receiver_tables, misfit[NT - 1])
    imaging_sum = adjoint_now * forward_list[NT - 1]
    adjoint_list = advance_all(
        adjoint_now,
        empty_field,
        [(receiver_tables, misfit[NT - 1 - adjoint_step]) for adjoint_step in range(1, NT)],
    )
    for position, wavefield in enumerate(adjoint_list):
        imaging_sum = imaging_sum + wavefield * forward_list[NT - 2 - position]
    period_count = device_count // PIECES
    slab_rows = piece_rows // period_count
    period_index = device_index // PIECES
    blocks = imaging_sum.reshape(period_count, slab_rows, span_y, span_z)

    def take_block(block_index):
        return lax.dynamic_index_in_dim(blocks, block_index % period_count, 0, keepdims=False)

    def cycle_step(step_index, carried):
        arrived = shifted_2(carried, "shot", PIECES)
        return arrived + take_block(period_index - 1 - step_index + 2 * period_count)

    start_block = take_block(period_index - 1 + period_count)
    return lax.fori_loop(1, period_count, cycle_step, start_block)


def solution(mesh):
    return jax.shard_map(
        per_device,
        mesh=mesh,
        in_specs=(
            P("groups", None, None),
            P(("groups", "shot"), None, None),
            P(("groups", "shot"), None, None),
            P(("groups", "shot"), None),
            P(("groups", "shot")),
            P(("groups", "shot")),
            P(("groups", "shot")),
            P(("groups", "shot"), None),
        ),
        out_specs=P(("groups", "shot"), None, None),
        check_vma=False,
    )
```

profile of v0, /device:TPU:0, one launch (start us, length us, event | category | flops | bytes accessed | tf_op | source)
XLA Modules:
  0.0 267.8 jit_solution(6011277250517265467)
XLA Ops:
  1.4 5.1 %collective-permute-start.1 = (f32[4,32,128]{2,1,0:T(8,128)S(1)}, f32[4,32,128]{2,1,0:T(8,128)S(1)}, u32[]{:S(2)}, u32[]{:S(2)}) collective-permute-start(f32[4,32,128]{2,1,0:T(8,128)S(1)} %get-tuple-element.404), channel_id=1, source_target_pairs={{1,0},{2,1},{3,2},{4,3},{5,4},{6,5},{7,6},{8,7},{9,8},{10,9},{11,1... | collective-permute-start | bytes 196616 | tf_op jit(solution)/shard_map/ppermute | solution.py:23
  35.2 4.5 %collective-permute-done.4 = f32[4,32,128]{2,1,0:T(8,128)S(1)} collective-permute-done((f32[4,32,128]{2,1,0:T(8,128)S(1)}, f32[4,32,128]{2,1,0:T(8,128)S(1)}, u32[]{:S(2)}, u32[]{:S(2)}) %collective-permute-start.4) | collective-permute-done | bytes 65568 | tf_op jit(solution)/shard_map/ppermute | solution.py:21
  49.2 4.6 %collective-permute-done.6 = f32[4,32,128]{2,1,0:T(8,128)S(1)} collective-permute-done((f32[4,32,128]{2,1,0:T(8,128)S(1)}, f32[4,32,128]{2,1,0:T(8,128)S(1)}, u32[]{:S(2)}, u32[]{:S(2)}) %collective-permute-start.6) | collective-permute-done | bytes 65568 | tf_op jit(solution)/shard_map/ppermute | solution.py:21
  64.0 4.6 %collective-permute-done.8 = f32[4,32,128]{2,1,0:T(8,128)S(1)} collective-permute-done((f32[4,32,128]{2,1,0:T(8,128)S(1)}, f32[4,32,128]{2,1,0:T(8,128)S(1)}, u32[]{:S(2)}, u32[]{:S(2)}) %collective-permute-start.8) | collective-permute-done | bytes 65568 | tf_op jit(solution)/shard_map/ppermute | solution.py:21
  77.1 4.4 %collective-permute-start.9 = (f32[4,32,128]{2,1,0:T(8,128)S(1)}, f32[4,32,128]{2,1,0:T(8,128)S(1)}, u32[]{:S(2)}, u32[]{:S(2)}) collective-permute-start(f32[4,32,128]{2,1,0:T(8,128)S(1)} %get-tuple-element.332), channel_id=1, source_target_pairs={{1,0},{2,1},{3,2},{4,3},{5,4},{6,5},{7,6},{8,7},{9,8},{10,9},{11,1... | collective-permute-start | bytes 196616 | tf_op jit(solution)/shard_map/ppermute | solution.py:23
  92.6 4.5 %collective-permute-start.11 = (f32[4,32,128]{2,1,0:T(8,128)S(1)}, f32[4,32,128]{2,1,0:T(8,128)S(1)}, u32[]{:S(2)}, u32[]{:S(2)}) collective-permute-start(f32[4,32,128]{2,1,0:T(8,128)S(1)} %get-tuple-element.314), channel_id=1, source_target_pairs={{1,0},{2,1},{3,2},{4,3},{5,4},{6,5},{7,6},{8,7},{9,8},{10,9},{11,1... | collective-permute-start | bytes 196616 | tf_op jit(solution)/shard_map/ppermute | solution.py:23
  99.0 4.5 %collective-permute-done.12 = f32[4,32,128]{2,1,0:T(8,128)S(1)} collective-permute-done((f32[4,32,128]{2,1,0:T(8,128)S(1)}, f32[4,32,128]{2,1,0:T(8,128)S(1)}, u32[]{:S(2)}, u32[]{:S(2)}) %collective-permute-start.12) | collective-permute-done | bytes 65568 | tf_op jit(solution)/shard_map/ppermute | solution.py:21
  114.8 4.7 %collective-permute-done.14 = f32[4,32,128]{2,1,0:T(8,128)S(1)} collective-permute-done((f32[4,32,128]{2,1,0:T(8,128)S(1)}, f32[4,32,128]{2,1,0:T(8,128)S(1)}, u32[]{:S(2)}, u32[]{:S(2)}) %collective-permute-start.14) | collective-permute-done | bytes 65568 | tf_op jit(solution)/shard_map/ppermute | solution.py:21
  131.6 4.6 %collective-permute-done.16 = f32[4,32,128]{2,1,0:T(8,128)S(1)} collective-permute-done((f32[4,32,128]{2,1,0:T(8,128)S(1)}, f32[4,32,128]{2,1,0:T(8,128)S(1)}, u32[]{:S(2)}, u32[]{:S(2)}) %collective-permute-start.16) | collective-permute-done | bytes 65568 | tf_op jit(solution)/shard_map/ppermute | solution.py:21
  136.2 2.7 %fusion.254 = f32[16,32,128]{2,1,0:T(8,128)S(1)} fusion(f32[16,32,128]{2,1,0:T(8,128)S(1)} %fusion.285, f32[4,32,128]{2,1,0:T(8,128)S(1)} %collective-permute-done.16, f32[4,32,128]{2,1,0:T(8,128)S(1)} %collective-permute-done.15, f32[16,32,124]{2,1,0:T(8,128)} %get-tuple-element.277, f32[16,32,124]{2,1,0:T(8,128)} %get-tuple-element.276, ...), kind=kLoop, calls=%fused_computation.433 | loop fusion | flops 2818048 | bytes 5171716 | tf_op jit(solution)/shard_map/add | solution.py:87
  141.7 9.0 %all_to_all.21 = f32[16,1,128]{2,1,0:T(1,128)S(1)} all-to-all(f32[16,1,128]{2,1,0:T(1,128)S(1)} %all_to_all.14), channel_id=1, replica_groups=mesh['groups'=2,'shot'=16] {'shot'}, dimensions={0} | all-to-all | bytes 16384 | tf_op jit(solution)/shard_map/all_to_all | solution.py:143
  151.3 3.5 %all-to-all-start.1 = ((f32[16,1,128]{2,1,0:T(1,128)}), f32[16,1,128]{2,1,0:T(1,128)S(1)}, u32[]{:S(2)}, u32[]{:S(2)}) async-start(f32[16,1,128]{2,1,0:T(1,128)} %bitcast.23), calls=%async_computation.1 | async-start | bytes 16384 | tf_op jit(solution)/shard_map/all_to_all | solution.py:144
  154.8 6.3 %all-to-all-done.1 = f32[16,1,128]{2,1,0:T(1,128)S(1)} async-done(((f32[16,1,128]{2,1,0:T(1,128)}), f32[16,1,128]{2,1,0:T(1,128)S(1)}, u32[]{:S(2)}, u32[]{:S(2)}) %all-to-all-start.1) | async-done | bytes 8224 | tf_op jit(solution)/shard_map/all_to_all | solution.py:144
  197.4 4.0 %collective-permute-start.19 = (f32[4,32,128]{2,1,0:T(8,128)S(1)}, f32[4,32,128]{2,1,0:T(8,128)S(1)}, u32[]{:S(2)}, u32[]{:S(2)}) collective-permute-start(f32[4,32,128]{2,1,0:T(8,128)S(1)} %get-tuple-element.242), channel_id=1, source_target_pairs={{1,0},{2,1},{3,2},{4,3},{5,4},{6,5},{7,6},{8,7},{9,8},{10,9},{11,1... | collective-permute-start | bytes 196616 | tf_op jit(solution)/shard_map/ppermute | solution.py:23
  203.3 4.5 %collective-permute-done.20 = f32[4,32,128]{2,1,0:T(8,128)S(1)} collective-permute-done((f32[4,32,128]{2,1,0:T(8,128)S(1)}, f32[4,32,128]{2,1,0:T(8,128)S(1)}, u32[]{:S(2)}, u32[]{:S(2)}) %collective-permute-start.20) | collective-permute-done | bytes 65568 | tf_op jit(solution)/shard_map/ppermute | solution.py:21
  211.1 4.6 %collective-permute-done.22 = f32[4,32,128]{2,1,0:T(8,128)S(1)} collective-permute-done((f32[4,32,128]{2,1,0:T(8,128)S(1)}, f32[4,32,128]{2,1,0:T(8,128)S(1)}, u32[]{:S(2)}, u32[]{:S(2)}) %collective-permute-start.22) | collective-permute-done | bytes 65568 | tf_op jit(solution)/shard_map/ppermute | solution.py:21
  218.9 4.6 %collective-permute-done.24 = f32[4,32,128]{2,1,0:T(8,128)S(1)} collective-permute-done((f32[4,32,128]{2,1,0:T(8,128)S(1)}, f32[4,32,128]{2,1,0:T(8,128)S(1)}, u32[]{:S(2)}, u32[]{:S(2)}) %collective-permute-start.24) | collective-permute-done | bytes 65568 | tf_op jit(solution)/shard_map/ppermute | solution.py:21
  226.8 4.5 %collective-permute-done.26 = f32[4,32,128]{2,1,0:T(8,128)S(1)} collective-permute-done((f32[4,32,128]{2,1,0:T(8,128)S(1)}, f32[4,32,128]{2,1,0:T(8,128)S(1)}, u32[]{:S(2)}, u32[]{:S(2)}) %collective-permute-start.26) | collective-permute-done | bytes 65568 | tf_op jit(solution)/shard_map/ppermute | solution.py:21
  234.6 4.5 %collective-permute-done.28 = f32[4,32,128]{2,1,0:T(8,128)S(1)} collective-permute-done((f32[4,32,128]{2,1,0:T(8,128)S(1)}, f32[4,32,128]{2,1,0:T(8,128)S(1)}, u32[]{:S(2)}, u32[]{:S(2)}) %collective-permute-start.28) | collective-permute-done | bytes 65568 | tf_op jit(solution)/shard_map/ppermute | solution.py:21
  242.4 4.5 %collective-permute-done.30 = f32[4,32,128]{2,1,0:T(8,128)S(1)} collective-permute-done((f32[4,32,128]{2,1,0:T(8,128)S(1)}, f32[4,32,128]{2,1,0:T(8,128)S(1)}, u32[]{:S(2)}, u32[]{:S(2)}) %collective-permute-start.30) | collective-permute-done | bytes 65568 | tf_op jit(solution)/shard_map/ppermute | solution.py:21
  248.0 18.5 %while.15 = (s32[]{:T(128)}, f32[4,32,128]{2,1,0:T(8,128)S(1)}, s32[]{:T(128)}, f32[4,4,32,128]{3,2,1,0:T(8,128)S(1)}, s32[]{:T(128)}, /*index=5*/s32[]{:T(128)}, s32[]{:T(128)}, s32[]{:T(128)}, s32[]{:T(128)}) while((s32[]{:T(128)}, f32[4,32,128]{2,1,0:T(8,128)S(1)}, s32[]{:T(128)}, f32[4,4,32,128]{3,2,1,0:T(8,128)S(1)}, s32[]{:T(128)}, ...), condition=%wide.region_9.10_spmd, body=%wide.region_8.9_spmd.sunk | while | flops 16402 | bytes 459056 | solution.py:171
  248.1 6.1 %collective-permute-done = f32[4,32,128]{2,1,0:T(8,128)S(1)} collective-permute-done((f32[4,32,128]{2,1,0:T(8,128)S(1)}, f32[4,32,128]{2,1,0:T(8,128)S(1)}, u32[]{:S(2)}, u32[]{:S(2)}) %collective-permute-start) | collective-permute-done | bytes 65568 | tf_op jit(solution)/shard_map/while/body/eval_jaxpr/ppermute | solution.py:33
  254.3 6.0 %collective-permute-done = f32[4,32,128]{2,1,0:T(8,128)S(1)} collective-permute-done((f32[4,32,128]{2,1,0:T(8,128)S(1)}, f32[4,32,128]{2,1,0:T(8,128)S(1)}, u32[]{:S(2)}, u32[]{:S(2)}) %collective-permute-start) | collective-permute-done | bytes 65568 | tf_op jit(solution)/shard_map/while/body/eval_jaxpr/ppermute | solution.py:33
  260.5 6.0 %collective-permute-done = f32[4,32,128]{2,1,0:T(8,128)S(1)} collective-permute-done((f32[4,32,128]{2,1,0:T(8,128)S(1)}, f32[4,32,128]{2,1,0:T(8,128)S(1)}, u32[]{:S(2)}, u32[]{:S(2)}) %collective-permute-start) | collective-permute-done | bytes 65568 | tf_op jit(solution)/shard_map/while/body/eval_jaxpr/ppermute | solution.py:33
  (342 shorter events, 153.9 us)
Async XLA Ops:
  0.9 23.8 %collective-permute-start.2 = (f32[4,32,128]{2,1,0:T(8,128)S(1)}, f32[4,32,128]{2,1,0:T(8,128)S(1)}, u32[]{:S(2)}, u32[]{:S(2)}) collective-permute-start(f32[4,32,128]{2,1,0:T(8,128)S(1)} %get-tuple-element.405), channel_id=1, source_target_pairs={{0,1},{1,2},{2,3},{3,4},{4,5},{5,6},{6,7},{7,8},{8,9},{9,10},{10,1... | collective-permute-start | bytes 196616 | tf_op jit(solution)/shard_map/ppermute | solution.py:21
  1.4 23.4 %collective-permute-start.1 = (f32[4,32,128]{2,1,0:T(8,128)S(1)}, f32[4,32,128]{2,1,0:T(8,128)S(1)}, u32[]{:S(2)}, u32[]{:S(2)}) collective-permute-start(f32[4,32,128]{2,1,0:T(8,128)S(1)} %get-tuple-element.404), channel_id=1, source_target_pairs={{1,0},{2,1},{3,2},{4,3},{5,4},{6,5},{7,6},{8,7},{9,8},{10,9},{11,1... | collective-permute-start | bytes 196616 | tf_op jit(solution)/shard_map/ppermute | solution.py:23
  33.3 6.4 %collective-permute-start.4 = (f32[4,32,128]{2,1,0:T(8,128)S(1)}, f32[4,32,128]{2,1,0:T(8,128)S(1)}, u32[]{:S(2)}, u32[]{:S(2)}) collective-permute-start(f32[4,32,128]{2,1,0:T(8,128)S(1)} %get-tuple-element.387), channel_id=1, source_target_pairs={{0,1},{1,2},{2,3},{3,4},{4,5},{5,6},{6,7},{7,8},{8,9},{9,10},{10,1... | collective-permute-start | bytes 196616 | tf_op jit(solution)/shard_map/ppermute | solution.py:21
  47.3 6.4 %collective-permute-start.6 = (f32[4,32,128]{2,1,0:T(8,128)S(1)}, f32[4,32,128]{2,1,0:T(8,128)S(1)}, u32[]{:S(2)}, u32[]{:S(2)}) collective-permute-start(f32[4,32,128]{2,1,0:T(8,128)S(1)} %get-tuple-element.369), channel_id=1, source_target_pairs={{0,1},{1,2},{2,3},{3,4},{4,5},{5,6},{6,7},{7,8},{8,9},{9,10},{10,1... | collective-permute-start | bytes 196616 | tf_op jit(solution)/shard_map/ppermute | solution.py:21
  62.1 6.4 %collective-permute-start.8 = (f32[4,32,128]{2,1,0:T(8,128)S(1)}, f32[4,32,128]{2,1,0:T(8,128)S(1)}, u32[]{:S(2)}, u32[]{:S(2)}) collective-permute-start(f32[4,32,128]{2,1,0:T(8,128)S(1)} %get-tuple-element.351), channel_id=1, source_target_pairs={{0,1},{1,2},{2,3},{3,4},{4,5},{5,6},{6,7},{7,8},{8,9},{9,10},{10,1... | collective-permute-start | bytes 196616 | tf_op jit(solution)/shard_map/ppermute | solution.py:21
  77.0 6.4 %collective-permute-start.10 = (f32[4,32,128]{2,1,0:T(8,128)S(1)}, f32[4,32,128]{2,1,0:T(8,128)S(1)}, u32[]{:S(2)}, u32[]{:S(2)}) collective-permute-start(f32[4,32,128]{2,1,0:T(8,128)S(1)} %get-tuple-element.333), channel_id=1, source_target_pairs={{0,1},{1,2},{2,3},{3,4},{4,5},{5,6},{6,7},{7,8},{8,9},{9,10},{10,1... | collective-permute-start | bytes 196616 | tf_op jit(solution)/shard_map/ppermute | solution.py:21
  77.1 6.4 %collective-permute-start.9 = (f32[4,32,128]{2,1,0:T(8,128)S(1)}, f32[4,32,128]{2,1,0:T(8,128)S(1)}, u32[]{:S(2)}, u32[]{:S(2)}) collective-permute-start(f32[4,32,128]{2,1,0:T(8,128)S(1)} %get-tuple-element.332), channel_id=1, source_target_pairs={{1,0},{2,1},{3,2},{4,3},{5,4},{6,5},{7,6},{8,7},{9,8},{10,9},{11,1... | collective-permute-start | bytes 196616 | tf_op jit(solution)/shard_map/ppermute | solution.py:23
  92.6 6.4 %collective-permute-start.11 = (f32[4,32,128]{2,1,0:T(8,128)S(1)}, f32[4,32,128]{2,1,0:T(8,128)S(1)}, u32[]{:S(2)}, u32[]{:S(2)}) collective-permute-start(f32[4,32,128]{2,1,0:T(8,128)S(1)} %get-tuple-element.314), channel_id=1, source_target_pairs={{1,0},{2,1},{3,2},{4,3},{5,4},{6,5},{7,6},{8,7},{9,8},{10,9},{11,1... | collective-permute-start | bytes 196616 | tf_op jit(solution)/shard_map/ppermute | solution.py:23
  97.1 6.4 %collective-permute-start.12 = (f32[4,32,128]{2,1,0:T(8,128)S(1)}, f32[4,32,128]{2,1,0:T(8,128)S(1)}, u32[]{:S(2)}, u32[]{:S(2)}) collective-permute-start(f32[4,32,128]{2,1,0:T(8,128)S(1)} %get-tuple-element.315), channel_id=1, source_target_pairs={{0,1},{1,2},{2,3},{3,4},{4,5},{5,6},{6,7},{7,8},{8,9},{9,10},{10,1... | collective-permute-start | bytes 196616 | tf_op jit(solution)/shard_map/ppermute | solution.py:21
  112.9 6.6 %collective-permute-start.14 = (f32[4,32,128]{2,1,0:T(8,128)S(1)}, f32[4,32,128]{2,1,0:T(8,128)S(1)}, u32[]{:S(2)}, u32[]{:S(2)}) collective-permute-start(f32[4,32,128]{2,1,0:T(8,128)S(1)} %get-tuple-element.297), channel_id=1, source_target_pairs={{0,1},{1,2},{2,3},{3,4},{4,5},{5,6},{6,7},{7,8},{8,9},{9,10},{10,1... | collective-permute-start | bytes 196616 | tf_op jit(solution)/shard_map/ppermute | solution.py:21
  129.7 6.4 %collective-permute-start.16 = (f32[4,32,128]{2,1,0:T(8,128)S(1)}, f32[4,32,128]{2,1,0:T(8,128)S(1)}, u32[]{:S(2)}, u32[]{:S(2)}) collective-permute-start(f32[4,32,128]{2,1,0:T(8,128)S(1)} %get-tuple-element.279), channel_id=1, source_target_pairs={{0,1},{1,2},{2,3},{3,4},{4,5},{5,6},{6,7},{7,8},{8,9},{9,10},{10,1... | collective-permute-start | bytes 196616 | tf_op jit(solution)/shard_map/ppermute | solution.py:21
  151.3 9.8 %all-to-all-start.1 = ((f32[16,1,128]{2,1,0:T(1,128)}), f32[16,1,128]{2,1,0:T(1,128)S(1)}, u32[]{:S(2)}, u32[]{:S(2)}) async-start(f32[16,1,128]{2,1,0:T(1,128)} %bitcast.23), calls=%async_computation.1 | async-start | bytes 16384 | tf_op jit(solution)/shard_map/all_to_all | solution.py:144
  171.4 22.7 %collective-permute-start.17 = (f32[4,32,128]{2,1,0:T(8,128)}, f32[4,32,128]{2,1,0:T(8,128)S(1)}, u32[]{:S(2)}, u32[]{:S(2)}) collective-permute-start(f32[4,32,128]{2,1,0:T(8,128)} %bitcast.26), channel_id=1, source_target_pairs={{1,0},{2,1},{3,2},{4,3},{5,4},{6,5},{7,6},{8,7},{9,8},{10,9},{11,1... | collective-permute-start | bytes 196616 | tf_op jit(solution)/shard_map/ppermute | solution.py:23
  171.4 22.7 %collective-permute-start.18 = (f32[4,32,128]{2,1,0:T(8,128)}, f32[4,32,128]{2,1,0:T(8,128)S(1)}, u32[]{:S(2)}, u32[]{:S(2)}) collective-permute-start(f32[4,32,128]{2,1,0:T(8,128)} %bitcast.27), channel_id=1, source_target_pairs={{0,1},{1,2},{2,3},{3,4},{4,5},{5,6},{6,7},{7,8},{8,9},{9,10},{10,1... | collective-permute-start | bytes 196616 | tf_op jit(solution)/shard_map/ppermute | solution.py:21
  197.4 5.9 %collective-permute-start.19 = (f32[4,32,128]{2,1,0:T(8,128)S(1)}, f32[4,32,128]{2,1,0:T(8,128)S(1)}, u32[]{:S(2)}, u32[]{:S(2)}) collective-permute-start(f32[4,32,128]{2,1,0:T(8,128)S(1)} %get-tuple-element.242), channel_id=1, source_target_pairs={{1,0},{2,1},{3,2},{4,3},{5,4},{6,5},{7,6},{8,7},{9,8},{10,9},{11,1... | collective-permute-start | bytes 196616 | tf_op jit(solution)/shard_map/ppermute | solution.py:23
  201.4 6.5 %collective-permute-start.20 = (f32[4,32,128]{2,1,0:T(8,128)S(1)}, f32[4,32,128]{2,1,0:T(8,128)S(1)}, u32[]{:S(2)}, u32[]{:S(2)}) collective-permute-start(f32[4,32,128]{2,1,0:T(8,128)S(1)} %get-tuple-element.243), channel_id=1, source_target_pairs={{0,1},{1,2},{2,3},{3,4},{4,5},{5,6},{6,7},{7,8},{8,9},{9,10},{10,1... | collective-permute-start | bytes 196616 | tf_op jit(solution)/shard_map/ppermute | solution.py:21
  209.2 6.4 %collective-permute-start.22 = (f32[4,32,128]{2,1,0:T(8,128)S(1)}, f32[4,32,128]{2,1,0:T(8,128)S(1)}, u32[]{:S(2)}, u32[]{:S(2)}) collective-permute-start(f32[4,32,128]{2,1,0:T(8,128)S(1)} %get-tuple-element.225), channel_id=1, source_target_pairs={{0,1},{1,2},{2,3},{3,4},{4,5},{5,6},{6,7},{7,8},{8,9},{9,10},{10,1... | collective-permute-start | bytes 196616 | tf_op jit(solution)/shard_map/ppermute | solution.py:21
  217.0 6.4 %collective-permute-start.24 = (f32[4,32,128]{2,1,0:T(8,128)S(1)}, f32[4,32,128]{2,1,0:T(8,128)S(1)}, u32[]{:S(2)}, u32[]{:S(2)}) collective-permute-start(f32[4,32,128]{2,1,0:T(8,128)S(1)} %get-tuple-element.207), channel_id=1, source_target_pairs={{0,1},{1,2},{2,3},{3,4},{4,5},{5,6},{6,7},{7,8},{8,9},{9,10},{10,1... | collective-permute-start | bytes 196616 | tf_op jit(solution)/shard_map/ppermute | solution.py:21
  224.9 6.4 %collective-permute-start.26 = (f32[4,32,128]{2,1,0:T(8,128)S(1)}, f32[4,32,128]{2,1,0:T(8,128)S(1)}, u32[]{:S(2)}, u32[]{:S(2)}) collective-permute-start(f32[4,32,128]{2,1,0:T(8,128)S(1)} %get-tuple-element.189), channel_id=1, source_target_pairs={{0,1},{1,2},{2,3},{3,4},{4,5},{5,6},{6,7},{7,8},{8,9},{9,10},{10,1... | collective-permute-start | bytes 196616 | tf_op jit(solution)/shard_map/ppermute | solution.py:21
  232.7 6.4 %collective-permute-start.28 = (f32[4,32,128]{2,1,0:T(8,128)S(1)}, f32[4,32,128]{2,1,0:T(8,128)S(1)}, u32[]{:S(2)}, u32[]{:S(2)}) collective-permute-start(f32[4,32,128]{2,1,0:T(8,128)S(1)} %get-tuple-element.171), channel_id=1, source_target_pairs={{0,1},{1,2},{2,3},{3,4},{4,5},{5,6},{6,7},{7,8},{8,9},{9,10},{10,1... | collective-permute-start | bytes 196616 | tf_op jit(solution)/shard_map/ppermute | solution.py:21
  240.5 6.4 %collective-permute-start.30 = (f32[4,32,128]{2,1,0:T(8,128)S(1)}, f32[4,32,128]{2,1,0:T(8,128)S(1)}, u32[]{:S(2)}, u32[]{:S(2)}) collective-permute-start(f32[4,32,128]{2,1,0:T(8,128)S(1)} %get-tuple-element.153), channel_id=1, source_target_pairs={{0,1},{1,2},{2,3},{3,4},{4,5},{5,6},{6,7},{7,8},{8,9},{9,10},{10,1... | collective-permute-start | bytes 196616 | tf_op jit(solution)/shard_map/ppermute | solution.py:21
  248.0 6.2 %collective-permute-start = (f32[4,32,128]{2,1,0:T(8,128)S(1)}, f32[4,32,128]{2,1,0:T(8,128)S(1)}, u32[]{:S(2)}, u32[]{:S(2)}) collective-permute-start(f32[4,32,128]{2,1,0:T(8,128)S(1)} %get-tuple-element.453), channel_id=1, source_target_pairs={{0,4},{1,5},{2,6},{3,7},{4,8},{5,9},{6,10},{7,11},{8,12},{9,13},{1... | collective-permute-start | bytes 196616 | tf_op jit(solution)/shard_map/while/body/eval_jaxpr/ppermute | solution.py:33
  254.3 6.1 %collective-permute-start = (f32[4,32,128]{2,1,0:T(8,128)S(1)}, f32[4,32,128]{2,1,0:T(8,128)S(1)}, u32[]{:S(2)}, u32[]{:S(2)}) collective-permute-start(f32[4,32,128]{2,1,0:T(8,128)S(1)} %get-tuple-element.453), channel_id=1, source_target_pairs={{0,4},{1,5},{2,6},{3,7},{4,8},{5,9},{6,10},{7,11},{8,12},{9,13},{1... | collective-permute-start | bytes 196616 | tf_op jit(solution)/shard_map/while/body/eval_jaxpr/ppermute | solution.py:33
  260.4 6.1 %collective-permute-start = (f32[4,32,128]{2,1,0:T(8,128)S(1)}, f32[4,32,128]{2,1,0:T(8,128)S(1)}, u32[]{:S(2)}, u32[]{:S(2)}) collective-permute-start(f32[4,32,128]{2,1,0:T(8,128)S(1)} %get-tuple-element.453), channel_id=1, source_target_pairs={{0,4},{1,5},{2,6},{3,7},{4,8},{5,9},{6,10},{7,11},{8,12},{9,13},{1... | collective-permute-start | bytes 196616 | tf_op jit(solution)/shard_map/while/body/eval_jaxpr/ppermute | solution.py:33
  (49 other events, 129.1 us)
where the time goes:
time: 269 us; the launch traced here: 268 us
  local copies, waits for them, and re-layouts  88.9 us (33%)
  waiting for transfers between devices  88.1 us (33%)
  other arithmetic  33.2 us (12%)
  starting transfers between devices  28.4 us (11%)
  matrix products  18.3 us (7%)
  blocking collectives  8.98 us (3%)
    ppermute x15, waiting for transfers between devices, extended_2(): lax.ppermute(tail, axis, [(i, (i + 1) % count) for i in range(count)])  55.2 us
    slice x120, local copies, waits for them, and re-layouts, shifted(): lax.slice_in_dim(values, offset, length, axis=axis_pos)  53.9 us
    add x14, other arithmetic, inject(): return wavefield + added.reshape(wavefield.shape)  25.2 us
    ppermute x15, starting transfers between devices, extended_2(): lax.ppermute(head, axis, [((i + 1) % count, i) for i in range(count)])  19.4 us
    ppermute x3, waiting for transfers between devices, shifted_2(): return lax.ppermute(value, axis, pairs)  18.1 us
    dot_general x8, matrix products, inject(): lax.dot_general(weighted, col_table, (((0,), (0,)), ((), ())), precision=...  14.3 us
    mul x16, local copies, waits for them, and re-layouts, inject(): weighted = row_table * amounts[:, None]  12.8 us
    unnamed x80, local copies, waits for them, and re-layouts  10.6 us
  transfers between devices with their start and end apart: 34, of which 23 were waited for; matrix products, arithmetic and copies ran while one was open for 18% of the time, Pallas kernels for 0%

commit v1 on v0

v1 whole, which is shorter than its diff:
```python
import functools

import jax
import jax.numpy as jnp
from jax import lax
from jax.experimental import pallas as pl
from jax.experimental.pallas import tpu as pltpu
from jax.sharding import PartitionSpec as P

NT = 8
PIECES = 4
MESH = pl.DeviceIdType.MESH
PAD = 8

stencil_center = -205.0 / 72.0
stencil_weights = (8.0 / 5.0, -1.0 / 5.0, 8.0 / 315.0, -1.0 / 560.0)
RAD = len(stencil_weights)


def kernel(
    count,
    courant_ref,
    now_ref,
    before_ref,
    wavelet_ref,
    source_ref,
    receiver_ref,
    order_ref,
    observed_ref,
    out_ref,
    waves,
    adjoints,
    model,
    source_mask,
    hits,
    scattered,
    image,
    row_table,
    col_table,
    spread,
    trace_out,
    trace_in,
    parts,
    load_sem,
    halo_send,
    halo_recv,
    trace_send,
    trace_recv,
    part_send,
    part_recv,
):
    planes, span_y, span_z = now_ref.shape
    receivers = receiver_ref.shape[1]
    per_owner = receivers // count
    periods = count // PIECES
    slab = planes // periods
    rows = planes * span_y
    group = lax.axis_index("groups")
    me = lax.axis_index("shot")
    left = lax.rem(me + count - 1, count)
    right = lax.rem(me + 1, count)
    piece = lax.rem(me, PIECES)
    period = me // PIECES
    inner = pl.ds(PAD, span_y)
    own = pl.ds(RAD, planes)

    loads = [
        pltpu.make_async_copy(now_ref, waves.at[1, own, inner], load_sem.at[0]),
        pltpu.make_async_copy(before_ref, waves.at[0, own, inner], load_sem.at[1]),
        pltpu.make_async_copy(
            courant_ref.at[pl.ds(piece * planes, planes)], model, load_sem.at[2]
        ),
    ]
    for load in loads:
        load.start()

    barrier = pltpu.get_barrier_semaphore()

    def greet(step, carry):
        pl.semaphore_signal(
            barrier, inc=1, device_id=(group, lax.rem(me + step, count)), device_id_type=MESH
        )
        return carry

    lax.fori_loop(1, count, greet, 0)

    for d in range(count):
        trace_out[d] = observed_ref[d : d + 1, :]

    pl.semaphore_wait(barrier, count - 1)

    def halo(field, slot, exchange, side, source=None):
        first = RAD if side == 0 else planes
        target = planes + RAD if side == 0 else 0
        if source is None:
            source = field.at[slot, pl.ds(first, RAD), inner]
        return pltpu.make_async_remote_copy(
            src_ref=source,
            dst_ref=field.at[slot, pl.ds(target, RAD), inner],
            send_sem=halo_send.at[side, exchange],
            recv_sem=halo_recv.at[side, exchange],
            device_id=(group, left if side == 0 else right),
            device_id_type=MESH,
        )

    first_sends = [
        halo(waves, 1, 0, 0, now_ref.at[pl.ds(0, RAD)]),
        halo(waves, 1, 0, 1, now_ref.at[pl.ds(planes - RAD, RAD)]),
    ]
    for send in first_sends:
        send.start()

    def trace_copy(step):
        peer = lax.rem(me + step, count)
        return pltpu.make_async_remote_copy(
            src_ref=trace_out.at[peer],
            dst_ref=trace_in.at[me],
            send_sem=trace_send.at[step],
            recv_sem=trace_recv.at[step],
            device_id=(group, peer),
            device_id_type=MESH,
        )

    def trace_start(step, carry):
        trace_copy(step).start()
        return carry

    lax.fori_loop(1, count, trace_start, 0)
    own_trace = pltpu.make_async_copy(trace_out.at[me], trace_in.at[me], load_sem.at[3])
    own_trace.start()

    edge = jnp.zeros((planes, PAD, span_z), jnp.float32)

    def clear(slot, carry):
        waves[slot, own, pl.ds(0, PAD), :] = edge
        waves[slot, own, pl.ds(PAD + span_y, PAD), :] = edge
        adjoints[slot, own, pl.ds(0, PAD), :] = edge
        adjoints[slot, own, pl.ds(PAD + span_y, PAD), :] = edge
        return carry

    lax.fori_loop(0, NT + 1, clear, 0)
    adjoints[0, own, inner, :] = jnp.zeros((planes, span_y, span_z), jnp.float32)

    cell = source_ref[0]
    flat = lax.broadcasted_iota(jnp.int32, (rows, span_z), 0) * span_z + lax.broadcasted_iota(
        jnp.int32, (rows, span_z), 1
    )
    source_mask[...] = jnp.where(flat == cell, 1.0, 0.0)

    cells = receiver_ref[...]
    order = order_ref[...]
    down = lax.broadcasted_iota(jnp.int32, (receivers, receivers), 0)
    across = lax.broadcasted_iota(jnp.int32, (receivers, receivers), 1)
    same = down == across
    cells_col = jnp.sum(jnp.where(same, cells, 0), axis=1, keepdims=True)
    order_col = jnp.sum(jnp.where(same, order, 0), axis=1, keepdims=True)
    owned_row = jnp.sum(jnp.where(down == order, cells_col, 0), axis=0, keepdims=True)
    owned_col = jnp.sum(jnp.where(across == order_col, cells, 0), axis=1, keepdims=True)
    row_table[...] = jnp.where(
        owned_row // span_z == lax.broadcasted_iota(jnp.int32, (rows, receivers), 0), 1.0, 0.0
    ).astype(jnp.bfloat16)
    col_hot = jnp.where(
        lax.rem(owned_col, span_z) == lax.broadcasted_iota(jnp.int32, (receivers, span_z), 1),
        1.0,
        0.0,
    )
    col_table[...] = col_hot
    hits[...] = jnp.dot(
        row_table[...], col_hot.astype(jnp.bfloat16), preferred_element_type=jnp.float32
    )

    lane = lax.broadcasted_iota(jnp.int32, (1, span_z), 1)
    lane_weights = []
    for distance in range(1, RAD + 1):
        weight = stencil_weights[distance - 1]
        lane_weights.append(
            (
                jnp.where(lane >= distance, weight, 0.0),
                jnp.where(lane < span_z - distance, weight, 0.0),
            )
        )

    def advanced(field, now, plane):
        at = plane + RAD
        center = field[now, at, inner, :]
        total = (3.0 * stencil_center) * center
        for distance in range(1, RAD + 1):
            beside = field[now, at + distance, inner, :] + field[now, at - distance, inner, :]
            beside = beside + (
                field[now, at, pl.ds(PAD + distance, span_y), :]
                + field[now, at, pl.ds(PAD - distance, span_y), :]
            )
            up, low = lane_weights[distance - 1]
            total = total + stencil_weights[distance - 1] * beside
            total = total + (
                up * pltpu.roll(center, distance, 1)
                + low * pltpu.roll(center, span_z - distance, 1)
            )
        return 2.0 * center - field[now - 1, at, inner, :] + model[plane] * total

    def plane_rows(plane):
        return pl.ds(pl.multiple_of(plane * span_y, span_y), span_y)

    def forward_planes(step, start):
        amount = wavelet_ref[0, step]
        made = [
            advanced(waves, step + 1, start + i)
            + amount * source_mask[plane_rows(start + i), :]
            for i in range(RAD)
        ]
        for i in range(RAD):
            waves[step + 2, start + i + RAD, inner, :] = made[i]
        return made

    def sources(step, plane, wave):
        return hits[plane_rows(plane), :] * wave - scattered[step, plane_rows(plane), :]

    def adjoint_planes(step, start, size=RAD):
        made = []
        for i in range(size):
            plane = start + i
            wave = waves[NT + 1 - step, plane + RAD, inner, :]
            made.append(advanced(adjoints, step, plane) + sources(NT - 1 - step, plane, wave))
        return made

    last = planes - RAD
    middle = range(RAD, last, RAD)

    for load in loads:
        load.wait()

    def spread_traces():
        own_trace.wait()

        def arrived(step, carry):
            trace_copy(step).wait_recv()
            return carry

        lax.fori_loop(1, count, arrived, 0)
        repeated = jnp.broadcast_to(trace_in[...], (count, per_owner, span_z)).reshape(
            receivers, span_z
        )
        slot_of = lax.rem(lax.broadcasted_iota(jnp.int32, (receivers, span_z), 0), per_owner)
        lane_slot = lax.rem(lax.broadcasted_iota(jnp.int32, (receivers, span_z), 1), per_owner)
        spread[...] = jnp.where(slot_of == lane_slot, repeated, 0.0)

    lane_step = lax.broadcasted_iota(jnp.int32, (span_z, span_z), 0) // per_owner

    def scatter(step):
        chosen = jnp.where(lane_step == step, 1.0, 0.0)
        values = jnp.dot(
            spread[...],
            chosen,
            precision=lax.Precision.HIGHEST,
            preferred_element_type=jnp.float32,
        )
        weighted = col_table[...] * values
        total = None
        for _ in range(3):
            piece_of = weighted.astype(jnp.bfloat16)
            weighted = weighted - piece_of.astype(jnp.float32)
            term = jnp.dot(row_table[...], piece_of, preferred_element_type=jnp.float32)
            total = term if total is None else total + term
        scattered[step] = total

    spread_traces()

    def forward_step(step, carry):
        halo(waves, step + 1, step, 1).wait_recv()
        forward_planes(step, 0)
        halo(waves, step + 2, step + 1, 0).start()
        halo(waves, step + 1, step, 0).wait_recv()
        forward_planes(step, last)
        halo(waves, step + 2, step + 1, 1).start()
        for start in middle:
            forward_planes(step, start)
        scatter(step)
        return carry

    lax.fori_loop(0, NT - 1, forward_step, 0)
    scatter(NT - 1)

    def begin_adjoint(start):
        made = forward_planes(NT - 1, start)
        for i in range(RAD):
            adjoints[1, start + i + RAD, inner, :] = sources(NT - 1, start + i, made[i])

    halo(waves, NT, NT - 1, 1).wait_recv()
    begin_adjoint(0)
    halo(adjoints, 1, NT, 0).start()
    halo(waves, NT, NT - 1, 0).wait_recv()
    begin_adjoint(last)
    halo(adjoints, 1, NT, 1).start()
    for start in middle:
        begin_adjoint(start)
    for plane in range(planes):
        image[plane] = (
            adjoints[1, plane + RAD, inner, :] * waves[NT + 1, plane + RAD, inner, :]
        )

    def adjoint_step(step, carry):
        def keep(start):
            made = adjoint_planes(step, start)
            for i in range(RAD):
                adjoints[step + 1, start + i + RAD, inner, :] = made[i]

        halo(adjoints, step, NT - 1 + step, 1).wait_recv()
        keep(0)
        halo(adjoints, step + 1, NT + step, 0).start()
        halo(adjoints, step, NT - 1 + step, 0).wait_recv()
        keep(last)
        halo(adjoints, step + 1, NT + step, 1).start()
        for start in middle:
            keep(start)
        for plane in range(planes):
            image[plane] += (
                adjoints[step + 1, plane + RAD, inner, :]
                * waves[NT + 1 - step, plane + RAD, inner, :]
            )
        return carry

    lax.fori_loop(1, NT - 1, adjoint_step, 0)

    halo(adjoints, NT - 1, 2 * NT - 2, 1).wait_recv()
    halo(adjoints, NT - 1, 2 * NT - 2, 0).wait_recv()

    def part_copy(step):
        target = lax.rem(period + step, periods)
        return pltpu.make_async_remote_copy(
            src_ref=image.at[pl.ds(target * slab, slab)],
            dst_ref=parts.at[step],
            send_sem=part_send.at[step],
            recv_sem=part_recv.at[step],
            device_id=(group, target * PIECES + piece),
            device_id_type=MESH,
        )

    def finish(start):
        made = adjoint_planes(NT - 1, start, slab)
        return [
            image[start + i] + made[i] * waves[2, start + i + RAD, inner, :] for i in range(slab)
        ]

    def send_part(step, carry):
        start = lax.rem(period + step, periods) * slab
        made = finish(start)
        for i in range(slab):
            image[start + i] = made[i]
        part_copy(step).start()
        return carry

    lax.fori_loop(1, periods, send_part, 0)
    start = period * slab
    made = finish(start)

    for send in first_sends:
        send.wait_send()

    def sent_wave(step, carry):
        for side in range(2):
            halo(waves, step + 1, step, side).wait_send()
        return carry

    lax.fori_loop(1, NT, sent_wave, 0)

    def sent_adjoint(step, carry):
        for side in range(2):
            halo(adjoints, step, NT - 1 + step, side).wait_send()
        return carry

    lax.fori_loop(1, NT, sent_adjoint, 0)

    def sent_trace(step, carry):
        trace_copy(step).wait_send()
        return carry

    lax.fori_loop(1, count, sent_trace, 0)

    for i in range(slab):
        out_ref[i] = made[i]

    def add_part(step, carry):
        part_copy(step).wait_recv()
        out_ref[...] += parts[step]
        return carry

    lax.fori_loop(1, periods, add_part, 0)

    def sent_part(step, carry):
        part_copy(step).wait_send()
        return carry

    lax.fori_loop(1, periods, sent_part, 0)


def per_device(
    courant_sq, wave_now, wave_before, wavelet, source_cell, receiver_cell, send_order, observed
):
    count = lax.axis_size("shot")
    planes, span_y, span_z = wave_now.shape
    receivers = receiver_cell.shape[0]
    periods = count // PIECES
    slab = planes // periods
    rows = planes * span_y
    tall = (planes + 2 * RAD, span_y + 2 * PAD, span_z)
    anywhere = pl.BlockSpec(memory_space=pl.ANY)
    scalars = pl.BlockSpec(memory_space=pltpu.SMEM)
    vectors = pl.BlockSpec(memory_space=pltpu.VMEM)
    dma = pltpu.SemaphoreType.DMA
    return pl.pallas_call(
        functools.partial(kernel, count),
        out_shape=jax.ShapeDtypeStruct((slab, span_y, span_z), jnp.float32),
        in_specs=[
            anywhere,
            anywhere,
            anywhere,
            scalars,
            scalars,
            vectors,
            vectors,
            vectors,
        ],
        out_specs=vectors,
        scratch_shapes=[
            pltpu.VMEM((NT + 2,) + tall, jnp.float32),
            pltpu.VMEM((NT + 1,) + tall, jnp.float32),
            pltpu.VMEM((planes, span_y, span_z), jnp.float32),
            pltpu.VMEM((rows, span_z), jnp.float32),
            pltpu.VMEM((rows, span_z), jnp.float32),
            pltpu.VMEM((NT, rows, span_z), jnp.float32),
            pltpu.VMEM((planes, span_y, span_z), jnp.float32),
            pltpu.VMEM((rows, receivers), jnp.bfloat16),
            pltpu.VMEM((receivers, span_z), jnp.float32),
            pltpu.VMEM((receivers, span_z), jnp.float32),
            pltpu.VMEM((count, 1, span_z), jnp.float32),
            pltpu.VMEM((count, 1, span_z), jnp.float32),
            pltpu.VMEM((periods, slab, span_y, span_z), jnp.float32),
            dma((4,)),
            dma((2, 2 * NT - 1)),
            dma((2, 2 * NT - 1)),
            dma((count,)),
            dma((count,)),
            dma((periods,)),
            dma((periods,)),
        ],
        compiler_params=pltpu.CompilerParams(
            collective_id=0, has_side_effects=True, vmem_limit_bytes=40 * 1024 * 1024
        ),
    )(
        courant_sq,
        wave_now,
        wave_before,
        wavelet,
        source_cell,
        receiver_cell.reshape(1, receivers),
        send_order.reshape(1, receivers),
        observed,
    )


def solution(mesh):
    return jax.shard_map(
        per_device,
        mesh=mesh,
        in_specs=(
            P("groups", None, None),
            P(("groups", "shot"), None, None),
            P(("groups", "shot"), None, None),
            P(("groups", "shot"), None),
            P(("groups", "shot")),
            P(("groups", "shot")),
            P(("groups", "shot")),
            P(("groups", "shot"), None),
        ),
        out_specs=P(("groups", "shot"), None, None),
        check_vma=False,
    )
```

time: 269 us -> 82.5 us (0.31)
  waiting for transfers between devices: 88.1 us -> 0 us
  local copies, waits for them, and re-layouts: 88.9 us -> 5.13 us
  Pallas kernels: 0 us -> 76.5 us
  other arithmetic: 33.2 us -> 0 us
  starting transfers between devices: 28.4 us -> 0 us
  matrix products: 18.3 us -> 0 us
  blocking collectives: 8.98 us -> 0 us
    ppermute x33 -> x0, waiting for transfers between devices: 81.9 us -> none  [the longest x15 55.2 us: extended_2(): lax.ppermute(tail, axis, [(i, (i + 1) % count) for i in range(count)])]
    pallas_call x0 -> x1, Pallas kernels: none -> 76.5 us  [per_device(): pl.pallas_call(functools.partial(kernel, count), out_shape=jax.ShapeDtype...]
    slice x137 -> x0, local copies, waits for them, and re-layouts: 57.1 us -> none  [the longest x120 53.9 us: shifted(): lax.slice_in_dim(values, offset, length, axis=axis_pos)]
    add x18 -> x0, other arithmetic: 26.3 us -> none  [the longest x14 25.2 us: inject(): return wavefield + added.reshape(wavefield.shape)]
    ppermute x33 -> x0, starting transfers between devices: 24.9 us -> none  [the longest x15 19.4 us: extended_2(): lax.ppermute(head, axis, [((i + 1) % count, i) for i in range(count)])]
    dot_general x16 -> x0, matrix products: 18.3 us -> none  [the longest x8 14.3 us: inject(): lax.dot_general(weighted, col_table, (((0,), (0,)), ((), ())), precision=...]
    mul x16 -> x0, local copies, waits for them, and re-layouts: 12.8 us -> none  [inject(): weighted = row_table * amounts[:, None]]
    all_to_all x1 -> x0, blocking collectives: 8.98 us -> none  [per_device(): lax.all_to_all(packed, 'shot', split_axis=0, concat_axis=0, tiled=True)]
  transfers between devices with their start and end apart: 34 -> 0, of which waited for: 23 -> 0; matrix products, arithmetic and copies ran while one was open for 18% -> 0% of each run, Pallas kernels for 0% -> 0%
where the time goes in v1:
time: 82.5 us; the launch traced here: 82.3 us
  Pallas kernels  76.5 us (93%)
  local copies, waits for them, and re-layouts  5.13 us (6%)
    pallas_call x1, Pallas kernels, per_device(): pl.pallas_call(functools.partial(kernel, count), out_shape=jax.ShapeDtype...  76.5 us
    unnamed x15, local copies, waits for them, and re-layouts  5.13 us

profile of v1, /device:TPU:0, one launch (start us, length us, event | category | flops | bytes accessed | tf_op | source)
XLA Modules:
  0.0 82.3 jit_solution(9282252847876502940)
XLA Ops:
  0.7 0.0 copy-start.5
  0.7 0.0 copy-start.4
  0.7 0.0 copy-start.6
  0.7 0.7 copy-done.5
  1.3 0.0 copy-done.4
  1.3 0.0 copy-done.6
  1.4 0.0 copy-start
  1.4 1.2 %copy-done = f32[64,32,128]{2,1,0:T(8,128)S(1)} copy-done((f32[64,32,128]{2,1,0:T(8,128)S(1)}, f32[64,32,128]{2,1,0:T(8,128)}, u32[]{:S(2)}) %copy-start) | copy-done | bytes 1048600
  2.6 0.0 copy-start.1
  2.6 0.9 %copy-done.1 = f32[16,32,128]{2,1,0:T(8,128)S(1)} copy-done((f32[16,32,128]{2,1,0:T(8,128)S(1)}, f32[16,32,128]{2,1,0:T(8,128)}, u32[]{:S(2)}) %copy-start.1) | copy-done | bytes 262168
  3.5 0.0 copy-start.2
  3.5 0.9 %copy-done.2 = f32[16,32,128]{2,1,0:T(8,128)S(1)} copy-done((f32[16,32,128]{2,1,0:T(8,128)S(1)}, f32[16,32,128]{2,1,0:T(8,128)}, u32[]{:S(2)}) %copy-start.2) | copy-done | bytes 262168
  4.5 0.0 copy-start.3
  4.5 0.7 copy-done.3
  5.2 76.5 %shard_map.82 = f32[4,32,128]{2,1,0:T(8,128)S(1)} custom-call(f32[64,32,128]{2,1,0:T(8,128)S(1)} %copy-done, f32[16,32,128]{2,1,0:T(8,128)S(1)} %copy-done.1, f32[16,32,128]{2,1,0:T(8,128)S(1)} %copy-done.2, f32[1,8]{1,0:T(1,128)S(1)} %copy-done.6, s32[1]{0:T(128)S(6)} %copy.10.source_ref, s32[1,256]{1,0:T(1,128)S(1)} %bitcast.2, s32[1,256]{1,0:T(1,128)S(1)} %bitcast.3, ...), custom_call_target="tpu_custom_call" | custom-call | tf_op jit(solution)/shard_map/pallas_call | solution.py:410
  81.6 0.6 copy.11
Async XLA Ops:
  0.7 0.7 copy-start.5
  0.7 0.7 copy-start.4
  0.7 0.7 copy-start.6
  1.4 1.2 %copy-start = (f32[64,32,128]{2,1,0:T(8,128)S(1)}, f32[64,32,128]{2,1,0:T(8,128)}, u32[]{:S(2)}) copy-start(f32[64,32,128]{2,1,0:T(8,128)} %courant_ref.1) | copy-start | bytes 3145732
  2.6 0.9 %copy-start.1 = (f32[16,32,128]{2,1,0:T(8,128)S(1)}, f32[16,32,128]{2,1,0:T(8,128)}, u32[]{:S(2)}) copy-start(f32[16,32,128]{2,1,0:T(8,128)} %now_ref.1) | copy-start | bytes 786436
  3.5 0.9 %copy-start.2 = (f32[16,32,128]{2,1,0:T(8,128)S(1)}, f32[16,32,128]{2,1,0:T(8,128)}, u32[]{:S(2)}) copy-start(f32[16,32,128]{2,1,0:T(8,128)} %before_ref.1) | copy-start | bytes 786436
  4.5 0.7 copy-start.3

commit v2 on v1

v2 whole, which is shorter than its diff:
```python
import functools

import jax
import jax.numpy as jnp
from jax import lax
from jax.experimental import pallas as pl
from jax.experimental.pallas import tpu as pltpu
from jax.sharding import PartitionSpec as P

NT = 8
PIECES = 4
MESH = pl.DeviceIdType.MESH
PAD = 8

stencil_center = -205.0 / 72.0
stencil_weights = (8.0 / 5.0, -1.0 / 5.0, 8.0 / 315.0, -1.0 / 560.0)
RAD = len(stencil_weights)
DEEP = 2 * RAD


def kernel(
    count,
    courant_ref,
    now_ref,
    before_ref,
    wavelet_ref,
    source_ref,
    receiver_ref,
    order_ref,
    observed_ref,
    out_ref,
    waves,
    adjoints,
    model,
    source_mask,
    source_note,
    hits,
    scattered,
    edge_out,
    edge_in,
    image,
    row_table,
    col_table,
    spread,
    observed,
    trace_out,
    trace_in,
    parts,
    load_sem,
    halo_send,
    halo_recv,
    first_send,
    first_recv,
    edge_send,
    edge_recv,
    trace_send,
    trace_recv,
    part_send,
    part_recv,
):
    planes, span_y, span_z = now_ref.shape
    receivers = receiver_ref.shape[1]
    per_owner = receivers // count
    periods = count // PIECES
    slab = planes // periods
    rows = planes * span_y
    model_planes = courant_ref.shape[0]
    group = lax.axis_index("groups")
    me = lax.axis_index("shot")
    left = lax.rem(me + count - 1, count)
    right = lax.rem(me + 1, count)
    piece = lax.rem(me, PIECES)
    period = me // PIECES
    inner = pl.ds(PAD, span_y)
    own = pl.ds(DEEP, planes)
    half = planes // 2

    barrier = pltpu.get_barrier_semaphore()

    def greet(step, carry):
        pl.semaphore_signal(
            barrier, inc=1, device_id=(group, lax.rem(me + step, count)), device_id_type=MESH
        )
        return carry

    lax.fori_loop(1, count, greet, 0)

    trace_load = pltpu.make_async_copy(observed_ref, observed, load_sem.at[6])
    trace_load.start()
    start_plane = piece * planes
    loads = [
        pltpu.make_async_copy(now_ref, waves.at[1, own, inner], load_sem.at[0]),
        pltpu.make_async_copy(before_ref, waves.at[0, own, inner], load_sem.at[1]),
        pltpu.make_async_copy(
            courant_ref.at[pl.ds(start_plane, planes)], model.at[pl.ds(RAD, planes)], load_sem.at[2]
        ),
        pltpu.make_async_copy(
            courant_ref.at[pl.ds(lax.rem(start_plane + model_planes - RAD, model_planes), RAD)],
            model.at[pl.ds(0, RAD)],
            load_sem.at[3],
        ),
        pltpu.make_async_copy(
            courant_ref.at[pl.ds(lax.rem(start_plane + planes, model_planes), RAD)],
            model.at[pl.ds(RAD + planes, RAD)],
            load_sem.at[4],
        ),
    ]
    for load in loads:
        load.start()

    for step in range(NT):
        source_note[1, step : step + 1, :] = jnp.full((1, span_z), wavelet_ref[0, step], jnp.float32)
    cell_value = source_ref[0].astype(jnp.float32)
    source_note[1, NT : 2 * NT, :] = jnp.full((NT, span_z), cell_value, jnp.float32)

    trace_load.wait()
    for d in range(count):
        trace_out[d] = observed[d : d + 1, :]

    def neighbour(side):
        return (group, lax.rem(me + count - 1 + 2 * side, count))

    def remote(source, target, send, recv, side):
        return pltpu.make_async_remote_copy(
            src_ref=source,
            dst_ref=target,
            send_sem=send,
            recv_sem=recv,
            device_id=neighbour(side),
            device_id_type=MESH,
        )

    def halo(field, slot, exchange, side, source=None):
        if source is None:
            source = field.at[slot, pl.ds(DEEP + half * side, DEEP), inner]
        return remote(
            source,
            field.at[slot, pl.ds((DEEP + planes) * (1 - side), DEEP), inner],
            halo_send.at[side, exchange],
            halo_recv.at[side, exchange],
            side,
        )

    def last_halo(side):
        return remote(
            adjoints.at[NT - 1, pl.ds(DEEP + (planes - RAD) * side, RAD), inner],
            adjoints.at[NT - 1, pl.ds(DEEP + planes - (planes + RAD) * side, RAD), inner],
            halo_send.at[side, NT - 1],
            halo_recv.at[side, NT - 1],
            side,
        )

    def first_halo(side):
        return halo(waves, 1, 0, side, now_ref.at[pl.ds(half * side, DEEP)])

    def before_halo(side):
        return remote(
            before_ref.at[pl.ds((planes - RAD) * side, RAD)],
            waves.at[0, pl.ds(DEEP + planes - (planes + RAD) * side, RAD), inner],
            first_send.at[side, 0],
            first_recv.at[side, 0],
            side,
        )

    def note_copy(side):
        return remote(
            source_note.at[1],
            source_note.at[2 - 2 * side],
            first_send.at[side, 1],
            first_recv.at[side, 1],
            side,
        )

    def edge_copy(which, side):
        return remote(
            edge_out.at[which, side],
            edge_in.at[which, 1 - side],
            edge_send.at[side, which],
            edge_recv.at[side, which],
            side,
        )

    def trace_copy(step):
        peer = lax.rem(me + step, count)
        return pltpu.make_async_remote_copy(
            src_ref=trace_out.at[peer],
            dst_ref=trace_in.at[me],
            send_sem=trace_send.at[step],
            recv_sem=trace_recv.at[step],
            device_id=(group, peer),
            device_id_type=MESH,
        )

    pl.semaphore_wait(barrier, count - 1)
    for side in range(2):
        first_halo(side).start()
    for side in range(2):
        before_halo(side).start()
        note_copy(side).start()

    def trace_start(step, carry):
        trace_copy(step).start()
        return carry

    lax.fori_loop(1, count, trace_start, 0)
    own_trace = pltpu.make_async_copy(trace_out.at[me], trace_in.at[me], load_sem.at[5])
    own_trace.start()

    wide = pl.ds(DEEP - RAD, planes + 2 * RAD)
    blank = jnp.zeros((planes + 2 * RAD, PAD, span_z), jnp.float32)

    def clear(slot, carry):
        waves[slot, wide, pl.ds(0, PAD), :] = blank
        waves[slot, wide, pl.ds(PAD + span_y, PAD), :] = blank
        adjoints[slot, wide, pl.ds(0, PAD), :] = blank
        adjoints[slot, wide, pl.ds(PAD + span_y, PAD), :] = blank
        return carry

    lax.fori_loop(0, NT, clear, 0)
    waves[NT, wide, pl.ds(0, PAD), :] = blank
    waves[NT, wide, pl.ds(PAD + span_y, PAD), :] = blank
    adjoints[0, wide, inner, :] = jnp.zeros((planes + 2 * RAD, span_y, span_z), jnp.float32)

    def cells_from(plane, size):
        shape = (size * span_y, span_z)
        flat = lax.broadcasted_iota(jnp.int32, shape, 0) * span_z
        flat = flat + lax.broadcasted_iota(jnp.int32, shape, 1) + plane * (span_y * span_z)
        return flat.astype(jnp.float32)

    def mark_source(place, size, plane, owner):
        marked = jnp.where(
            cells_from(plane, size) == source_note[owner, NT : NT + 1, :], 1.0, 0.0
        )
        source_mask[pl.ds(place, size)] = marked.reshape(size, span_y, span_z)

    mark_source(RAD, planes, 0, 1)

    cells = receiver_ref[...]
    order = order_ref[...]
    down = lax.broadcasted_iota(jnp.int32, (receivers, receivers), 0)
    across = lax.broadcasted_iota(jnp.int32, (receivers, receivers), 1)
    same = down == across
    cells_col = jnp.sum(jnp.where(same, cells, 0), axis=1, keepdims=True)
    order_col = jnp.sum(jnp.where(same, order, 0), axis=1, keepdims=True)
    owned_row = jnp.sum(jnp.where(down == order, cells_col, 0), axis=0, keepdims=True)
    owned_col = jnp.sum(jnp.where(across == order_col, cells, 0), axis=1, keepdims=True)
    row_table[...] = jnp.where(
        owned_row // span_z == lax.broadcasted_iota(jnp.int32, (rows, receivers), 0), 1.0, 0.0
    ).astype(jnp.bfloat16)
    col_hot = jnp.where(
        lax.rem(owned_col, span_z) == lax.broadcasted_iota(jnp.int32, (receivers, span_z), 1),
        1.0,
        0.0,
    )
    col_table[...] = col_hot
    hits[...] = jnp.dot(
        row_table[...], col_hot.astype(jnp.bfloat16), preferred_element_type=jnp.float32
    )

    lane = lax.broadcasted_iota(jnp.int32, (1, span_z), 1)
    lane_weights = []
    for distance in range(1, RAD + 1):
        weight = stencil_weights[distance - 1]
        lane_weights.append(
            (
                jnp.where(lane >= distance, weight, 0.0),
                jnp.where(lane < span_z - distance, weight, 0.0),
            )
        )

    def advanced(field, now, plane):
        at = plane + DEEP
        center = field[now, at, inner, :]
        total = (3.0 * stencil_center) * center
        for distance in range(1, RAD + 1):
            beside = field[now, at + distance, inner, :] + field[now, at - distance, inner, :]
            beside = beside + (
                field[now, at, pl.ds(PAD + distance, span_y), :]
                + field[now, at, pl.ds(PAD - distance, span_y), :]
            )
            up, low = lane_weights[distance - 1]
            total = total + stencil_weights[distance - 1] * beside
            total = total + (
                up * pltpu.roll(center, distance, 1)
                + low * pltpu.roll(center, span_z - distance, 1)
            )
        return 2.0 * center - field[now - 1, at, inner, :] + model[plane + RAD] * total

    def plane_rows(plane):
        return pl.ds(pl.multiple_of(plane * span_y, span_y), span_y)

    def store(field, slot, start, made):
        for i in range(len(made)):
            field[slot, start + i + DEEP, inner, :] = made[i]

    def forward_planes(step, start, owner=1):
        amount = source_note[owner, pl.ds(step, 1), :]
        made = [
            advanced(waves, step + 1, start + i) + amount * source_mask[start + i + RAD]
            for i in range(RAD)
        ]
        store(waves, step + 2, start, made)
        return made

    def sources(step, plane, wave):
        return hits[plane_rows(plane), :] * wave - scattered[step, plane_rows(plane), :]

    def adjoint_planes(step, start, size=RAD):
        made = []
        for i in range(size):
            plane = start + i
            wave = waves[NT + 1 - step, plane + DEEP, inner, :]
            made.append(advanced(adjoints, step, plane) + sources(NT - 1 - step, plane, wave))
        return made

    def adjoint_keep(step, start):
        store(adjoints, step + 1, start, adjoint_planes(step, start))

    def adjoint_beside(step, start, which, side):
        made = [
            advanced(adjoints, step, start + i) + edge_in[which, side, i] for i in range(RAD)
        ]
        store(adjoints, step + 1, start, made)

    def send_edges(which, step, side):
        start = (planes - RAD) * side
        for i in range(RAD):
            wave = waves[step + 2, start + i + DEEP, inner, :]
            edge_out[which, side, i] = sources(step, start + i, wave)
        edge_copy(which, side).start()

    middle = range(RAD, planes - RAD, RAD)

    def spread_traces():
        own_trace.wait()

        def arrived(step, carry):
            trace_copy(step).wait_recv()
            return carry

        lax.fori_loop(1, count, arrived, 0)
        repeated = jnp.broadcast_to(trace_in[...], (count, per_owner, span_z)).reshape(
            receivers, span_z
        )
        slot_of = lax.rem(lax.broadcasted_iota(jnp.int32, (receivers, span_z), 0), per_owner)
        lane_slot = lax.rem(lax.broadcasted_iota(jnp.int32, (receivers, span_z), 1), per_owner)
        spread[...] = jnp.where(slot_of == lane_slot, repeated, 0.0)

    lane_step = lax.broadcasted_iota(jnp.int32, (span_z, span_z), 0) // per_owner

    def scatter(step):
        chosen = jnp.where(lane_step == step, 1.0, 0.0)
        values = jnp.dot(
            spread[...],
            chosen,
            precision=lax.Precision.HIGHEST,
            preferred_element_type=jnp.float32,
        )
        weighted = col_table[...] * values
        total = None
        for _ in range(3):
            piece_of = weighted.astype(jnp.bfloat16)
            weighted = weighted - piece_of.astype(jnp.float32)
            term = jnp.dot(row_table[...], piece_of, preferred_element_type=jnp.float32)
            total = term if total is None else total + term
        scattered[step] = total

    for load in loads:
        load.wait()

    first_side = lax.rem(me, 2)

    def forward_pair(pair, begin_adjoint):
        step = 2 * pair
        for start in middle:
            forward_planes(step, start)

        def one_side(turn, carry):
            side = lax.rem(first_side + turn, 2)
            halo(waves, step + 1, pair, 1 - side).wait_recv()

            if not begin_adjoint:

                @pl.when(pair == 0)
                def _():
                    before_halo(1 - side).wait_recv()
                    note_copy(1 - side).wait_recv()
                    mark_source(
                        (planes + RAD) * side, RAD, (planes - RAD) * (1 - side), 2 * side
                    )

            forward_planes(step, (planes + RAD) * side - RAD, 2 * side)
            forward_planes(step, (planes - RAD) * side)
            for part in range(0, half, RAD):
                start = half * side + part
                made = forward_planes(step + 1, start)
                if begin_adjoint:
                    first = [
                        sources(NT - 1, start + i, made[i]) for i in range(RAD)
                    ]
                    store(adjoints, 1, start, first)
            if begin_adjoint:
                halo(adjoints, 1, NT // 2, side).start()
                send_edges(NT // 2 - 2, NT - 2, side)
            else:
                halo(waves, step + 3, pair + 1, side).start()
            return carry

        lax.fori_loop(0, 2, one_side, 0)

    def forward_loop(pair, carry):
        forward_pair(pair, False)

        @pl.when(pair == 0)
        def _():
            spread_traces()

        for i in range(3):
            scatter(3 * pair + i)

        @pl.when(pair > 0)
        def _():
            for side in range(2):
                send_edges(pair - 1, 2 * pair, side)

        return carry

    lax.fori_loop(0, NT // 2 - 1, forward_loop, 0)
    forward_pair(NT // 2 - 1, True)

    def add_image(step):
        for plane in range(planes):
            image[plane] += (
                adjoints[step, plane + DEEP, inner, :]
                * waves[NT + 2 - step, plane + DEEP, inner, :]
            )

    image[...] = jnp.zeros((planes, span_y, span_z), jnp.float32)

    def adjoint_pair(pair, last):
        step = 2 * pair + 1
        which = NT // 2 - 2 - pair
        for start in middle:
            adjoint_keep(step, start)

        def one_side(turn, carry):
            side = lax.rem(first_side + turn, 2)
            halo(adjoints, step, NT // 2 + pair, 1 - side).wait_recv()
            edge_copy(which, 1 - side).wait_recv()
            adjoint_beside(step, (planes + RAD) * side - RAD, which, side)
            adjoint_keep(step, (planes - RAD) * side)
            if last:
                adjoint_keep(step + 1, (planes - RAD) * side)
                last_halo(side).start()
            else:
                for part in range(0, half, RAD):
                    adjoint_keep(step + 1, half * side + part)
                halo(adjoints, step + 2, NT // 2 + pair + 1, side).start()
            return carry

        lax.fori_loop(0, 2, one_side, 0)
        if last:
            for start in middle:
                adjoint_keep(step + 1, start)
        add_image(step)
        add_image(step + 1)

    def adjoint_loop(pair, carry):
        adjoint_pair(pair, False)
        return carry

    lax.fori_loop(0, NT // 2 - 2, adjoint_loop, 0)
    adjoint_pair(NT // 2 - 2, True)
    add_image(NT - 1)

    for side in range(2):
        last_halo(side).wait_recv()

    def part_copy(step):
        target = lax.rem(period + step, periods)
        return pltpu.make_async_remote_copy(
            src_ref=image.at[pl.ds(target * slab, slab)],
            dst_ref=parts.at[step],
            send_sem=part_send.at[step],
            recv_sem=part_recv.at[step],
            device_id=(group, target * PIECES + piece),
            device_id_type=MESH,
        )

    def finish(start):
        made = adjoint_planes(NT - 1, start, slab)
        return [
            image[start + i] + made[i] * waves[2, start + i + DEEP, inner, :] for i in range(slab)
        ]

    def send_part(step, carry):
        start = lax.rem(period + step, periods) * slab
        made = finish(start)
        for i in range(slab):
            image[start + i] = made[i]
        part_copy(step).start()
        return carry

    lax.fori_loop(1, periods, send_part, 0)
    start = period * slab
    made = finish(start)
    for i in range(slab):
        out_ref[i] = made[i]

    for side in range(2):
        first_halo(side).wait_send()
        before_halo(side).wait_send()
        note_copy(side).wait_send()
        last_halo(side).wait_send()
        for pair in range(1, NT // 2):
            halo(waves, 2 * pair + 1, pair, side).wait_send()
            halo(adjoints, 2 * pair - 1, NT // 2 + pair - 1, side).wait_send()
            edge_copy(pair - 1, side).wait_send()

    def sent_trace(step, carry):
        trace_copy(step).wait_send()
        return carry

    lax.fori_loop(1, count, sent_trace, 0)

    def add_part(step, carry):
        part_copy(step).wait_recv()
        out_ref[...] += parts[step]
        return carry

    lax.fori_loop(1, periods, add_part, 0)

    def sent_part(step, carry):
        part_copy(step).wait_send()
        return carry

    lax.fori_loop(1, periods, sent_part, 0)


def per_device(
    courant_sq, wave_now, wave_before, wavelet, source_cell, receiver_cell, send_order, observed
):
    count = lax.axis_size("shot")
    planes, span_y, span_z = wave_now.shape
    receivers = receiver_cell.shape[0]
    periods = count // PIECES
    slab = planes // periods
    rows = planes * span_y
    tall = (planes + 2 * DEEP, span_y + 2 * PAD, span_z)
    anywhere = pl.BlockSpec(memory_space=pltpu.HBM)
    scalars = pl.BlockSpec(memory_space=pltpu.SMEM)
    vectors = pl.BlockSpec(memory_space=pltpu.VMEM)
    dma = pltpu.SemaphoreType.DMA
    return pl.pallas_call(
        functools.partial(kernel, count),
        out_shape=jax.ShapeDtypeStruct((slab, span_y, span_z), jnp.float32),
        in_specs=[
            anywhere,
            anywhere,
            anywhere,
            scalars,
            scalars,
            vectors,
            vectors,
            anywhere,
        ],
        out_specs=vectors,
        scratch_shapes=[
            pltpu.VMEM((NT + 2,) + tall, jnp.float32),
            pltpu.VMEM((NT,) + tall, jnp.float32),
            pltpu.VMEM((planes + 2 * RAD, span_y, span_z), jnp.float32),
            pltpu.VMEM((planes + 2 * RAD, span_y, span_z), jnp.float32),
            pltpu.VMEM((3, 2 * NT, span_z), jnp.float32),
            pltpu.VMEM((rows, span_z), jnp.float32),
            pltpu.VMEM((NT + 1, rows, span_z), jnp.float32),
            pltpu.VMEM((NT // 2 - 1, 2, RAD, span_y, span_z), jnp.float32),
            pltpu.VMEM((NT // 2 - 1, 2, RAD, span_y, span_z), jnp.float32),
            pltpu.VMEM((planes, span_y, span_z), jnp.float32),
            pltpu.VMEM((rows, receivers), jnp.bfloat16),
            pltpu.VMEM((receivers, span_z), jnp.float32),
            pltpu.VMEM((receivers, span_z), jnp.float32),
            pltpu.VMEM((count, span_z), jnp.float32),
            pltpu.VMEM((count, 1, span_z), jnp.float32),
            pltpu.VMEM((count, 1, span_z), jnp.float32),
            pltpu.VMEM((periods, slab, span_y, span_z), jnp.float32),
            dma((7,)),
            dma((2, NT)),
            dma((2, NT)),
            dma((2, 2)),
            dma((2, 2)),
            dma((2, NT // 2 - 1)),
            dma((2, NT // 2 - 1)),
            dma((count,)),
            dma((count,)),
            dma((periods,)),
            dma((periods,)),
        ],
        compiler_params=pltpu.CompilerParams(
            collective_id=0, has_side_effects=True, vmem_limit_bytes=63 * 1024 * 1024
        ),
    )(
        courant_sq,
        wave_now,
        wave_before,
        wavelet,
        source_cell,
        receiver_cell.reshape(1, receivers),
        send_order.reshape(1, receivers),
        observed,
    )


def solution(mesh):
    return jax.shard_map(
        per_device,
        mesh=mesh,
        in_specs=(
            P("groups", None, None),
            P(("groups", "shot"), None, None),
            P(("groups", "shot"), None, None),
            P(("groups", "shot"), None),
            P(("groups", "shot")),
            P(("groups", "shot")),
            P(("groups", "shot")),
            P(("groups", "shot"), None),
        ),
        out_specs=P(("groups", "shot"), None, None),
        check_vma=False,
    )
```

time: 82.5 us -> 59.2 us (0.72)
  Pallas kernels: 76.5 us -> 56.8 us
  local copies, waits for them, and re-layouts: 5.13 us -> 1.47 us
    pallas_call x1, Pallas kernels: 76.5 us -> 56.8 us  [per_device(): pl.pallas_call(functools.partial(kernel, count), out_shape=jax.ShapeDtype...]
    unnamed x15 -> x1, local copies, waits for them, and re-layouts: 5.13 us -> 1.47 us
where the time goes in v2:
time: 59.2 us; the launch traced here: 59 us
  Pallas kernels  56.8 us (96%)
  local copies, waits for them, and re-layouts  1.47 us (2%)
  between operations  0.66 us (1%)
    pallas_call x1, Pallas kernels, per_device(): pl.pallas_call(functools.partial(kernel, count), out_shape=jax.ShapeDtype...  56.8 us
    unnamed x1, local copies, waits for them, and re-layouts  1.47 us

profile of v2, /device:TPU:0, one launch (start us, length us, event | category | flops | bytes accessed | tf_op | source)
XLA Modules:
  0.0 59.0 jit_solution(3477277363643945047)
XLA Ops:
  0.7 56.8 %shard_map.82 = f32[4,32,128]{2,1,0:T(8,128)} custom-call(f32[64,32,128]{2,1,0:T(8,128)} %courant_ref.1, f32[16,32,128]{2,1,0:T(8,128)} %now_ref.1, f32[16,32,128]{2,1,0:T(8,128)} %before_ref.1, f32[1,8]{1,0:T(1,128)} %wavelet_ref.1, s32[1]{0:T(128)S(6)} %copy.10.source_ref, s32[1,256]{1,0:T(1,128)} %bitcast.2, s32[1,256]{1,0:T(1,128)} %bitcast.3, ...), custom_call_target="tpu_custom_call" | custom-call | tf_op jit(solution)/shard_map/pallas_call | solution.py:554
  57.5 1.5 %copy.11 = f32[4,32,128]{2,1,0:T(8,128)} copy(f32[4,32,128]{2,1,0:T(8,128)} %shard_map.82) | data formatting | bytes 131072

commit v3 on v2

--- a/solution.py
+++ b/solution.py
@@ -257,7 +257,7 @@
         row_table[...], col_hot.astype(jnp.bfloat16), preferred_element_type=jnp.float32
     )
 
-    lane = lax.broadcasted_iota(jnp.int32, (1, span_z), 1)
+    lane = lax.broadcasted_iota(jnp.int32, (1, 1, span_z), 2)
     lane_weights = []
     for distance in range(1, RAD + 1):
         weight = stencil_weights[distance - 1]
@@ -268,23 +268,36 @@
             )
         )
 
-    def advanced(field, now, plane):
-        at = plane + DEEP
-        center = field[now, at, inner, :]
-        total = (3.0 * stencil_center) * center
-        for distance in range(1, RAD + 1):
-            beside = field[now, at + distance, inner, :] + field[now, at - distance, inner, :]
-            beside = beside + (
-                field[now, at, pl.ds(PAD + distance, span_y), :]
-                + field[now, at, pl.ds(PAD - distance, span_y), :]
+    def advanced(field, now, start, size=RAD):
+        tiles = []
+        for row in range(0, span_y, PAD):
+            column = field[
+                now, pl.ds(start + DEEP - RAD, size + 2 * RAD), pl.ds(PAD + row, PAD), :
+            ]
+            here = pl.ds(start + DEEP, size)
+            center = column[RAD : RAD + size]
+            total = (3.0 * stencil_center) * center
+            for distance in range(1, RAD + 1):
+                beside = (
+                    column[RAD + distance : RAD + distance + size]
+                    + column[RAD - distance : RAD - distance + size]
+                )
+                beside = beside + (
+                    field[now, here, pl.ds(PAD + row + distance, PAD), :]
+                    + field[now, here, pl.ds(PAD + row - distance, PAD), :]
+                )
+                up, low = lane_weights[distance - 1]
+                total = total + stencil_weights[distance - 1] * beside
+                total = total + (
+                    up * pltpu.roll(center, distance, 2)
+                    + low * pltpu.roll(center, span_z - distance, 2)
+                )
+            tiles.append(
+                2.0 * center
+                - field[now - 1, here, pl.ds(PAD + row, PAD), :]
+                + model[pl.ds(start + RAD, size), pl.ds(row, PAD), :] * total
             )
-            up, low = lane_weights[distance - 1]
-            total = total + stencil_weights[distance - 1] * beside
-            total = total + (
-                up * pltpu.roll(center, distance, 1)
-                + low * pltpu.roll(center, span_z - distance, 1)
-            )
-        return 2.0 * center - field[now - 1, at, inner, :] + model[plane + RAD] * total
+        return jnp.concatenate(tiles, axis=1)
 
     def plane_rows(plane):
         return pl.ds(pl.multiple_of(plane * span_y, span_y), span_y)
@@ -295,10 +308,8 @@
 
     def forward_planes(step, start, owner=1):
         amount = source_note[owner, pl.ds(step, 1), :]
-        made = [
-            advanced(waves, step + 1, start + i) + amount * source_mask[start + i + RAD]
-            for i in range(RAD)
-        ]
+        ahead = advanced(waves, step + 1, start)
+        made = [ahead[i] + amount * source_mask[start + i + RAD] for i in range(RAD)]
         store(waves, step + 2, start, made)
         return made
 
@@ -307,19 +318,19 @@
 
     def adjoint_planes(step, start, size=RAD):
         made = []
+        ahead = advanced(adjoints, step, start, size)
         for i in range(size):
             plane = start + i
             wave = waves[NT + 1 - step, plane + DEEP, inner, :]
-            made.append(advanced(adjoints, step, plane) + sources(NT - 1 - step, plane, wave))
+            made.append(ahead[i] + sources(NT - 1 - step, plane, wave))
         return made
 
     def adjoint_keep(step, start):
         store(adjoints, step + 1, start, adjoint_planes(step, start))
 
     def adjoint_beside(step, start, which, side):
-        made = [
-            advanced(adjoints, step, start + i) + edge_in[which, side, i] for i in range(RAD)
-        ]
+        ahead = advanced(adjoints, step, start)
+        made = [ahead[i] + edge_in[which, side, i] for i in range(RAD)]
         store(adjoints, step + 1, start, made)
 
     def send_edges(which, step, side):
@@ -473,9 +484,6 @@
     adjoint_pair(NT // 2 - 2, True)
     add_image(NT - 1)
 
-    for side in range(2):
-        last_halo(side).wait_recv()
-
     def part_copy(step):
         target = lax.rem(period + step, periods)
         return pltpu.make_async_remote_copy(
@@ -493,19 +501,26 @@
             image[start + i] + made[i] * waves[2, start + i + DEEP, inner, :] for i in range(slab)
         ]
 
-    def send_part(step, carry):
-        start = lax.rem(period + step, periods) * slab
+    def send_part(which, carry):
+        start = which * slab
         made = finish(start)
         for i in range(slab):
             image[start + i] = made[i]
-        part_copy(step).start()
-        return carry
-
-    lax.fori_loop(1, periods, send_part, 0)
-    start = period * slab
-    made = finish(start)
+
+        @pl.when(which != period)
+        def _():
+            part_copy(lax.rem(which - period + periods, periods)).start()
+
+        return carry
+
+    low, high = RAD // slab, (planes - RAD) // slab
+    lax.fori_loop(low, high, send_part, 0)
+    for side in range(2):
+        last_halo(side).wait_recv()
+    lax.fori_loop(0, low, send_part, 0)
+    lax.fori_loop(high, periods, send_part, 0)
     for i in range(slab):
-        out_ref[i] = made[i]
+        out_ref[i] = image[period * slab + i]
 
     for side in range(2):
         first_halo(side).wait_send()

time: 59.2 us -> 58.3 us (0.985)
  Pallas kernels: 56.8 us -> 55.9 us
    pallas_call x1, Pallas kernels: 56.8 us -> 55.9 us  [per_device(): pl.pallas_call(functools.partial(kernel, count), out_shape=jax.ShapeDtype...]
where the time goes in v3:
time: 58.3 us; the launch traced here: 58.1 us
  Pallas kernels  55.9 us (96%)
  local copies, waits for them, and re-layouts  1.47 us (3%)
  between operations  0.66 us (1%)
    pallas_call x1, Pallas kernels, per_device(): pl.pallas_call(functools.partial(kernel, count), out_shape=jax.ShapeDtype...  55.9 us
    unnamed x1, local copies, waits for them, and re-layouts  1.47 us

profile of v3, /device:TPU:0, one launch (start us, length us, event | category | flops | bytes accessed | tf_op | source)
XLA Modules:
  0.0 58.1 jit_solution(16356080183550227734)
XLA Ops:
  0.7 55.9 %shard_map.82 = f32[4,32,128]{2,1,0:T(8,128)} custom-call(f32[64,32,128]{2,1,0:T(8,128)} %courant_ref.1, f32[16,32,128]{2,1,0:T(8,128)} %now_ref.1, f32[16,32,128]{2,1,0:T(8,128)} %before_ref.1, f32[1,8]{1,0:T(1,128)} %wavelet_ref.1, s32[1]{0:T(128)S(6)} %copy.10.source_ref, s32[1,256]{1,0:T(1,128)} %bitcast.2, s32[1,256]{1,0:T(1,128)} %bitcast.3, ...), custom_call_target="tpu_custom_call" | custom-call | tf_op jit(solution)/shard_map/pallas_call | solution.py:569
  56.6 1.5 %copy.11 = f32[4,32,128]{2,1,0:T(8,128)} copy(f32[4,32,128]{2,1,0:T(8,128)} %shard_map.82) | data formatting | bytes 131072

commit v4 on v3

--- a/solution.py
+++ b/solution.py
@@ -130,14 +130,14 @@
             device_id_type=MESH,
         )
 
-    def halo(field, slot, exchange, side, source=None):
+    def halo(field, slot, exchange, side, part, source=None):
         if source is None:
-            source = field.at[slot, pl.ds(DEEP + half * side, DEEP), inner]
+            source = field.at[slot, pl.ds(DEEP + half * side + part, RAD), inner]
         return remote(
             source,
-            field.at[slot, pl.ds((DEEP + planes) * (1 - side), DEEP), inner],
-            halo_send.at[side, exchange],
-            halo_recv.at[side, exchange],
+            field.at[slot, pl.ds((DEEP + planes) * (1 - side) + part, RAD), inner],
+            halo_send.at[part // RAD, side, exchange],
+            halo_recv.at[part // RAD, side, exchange],
             side,
         )
 
@@ -145,13 +145,13 @@
         return remote(
             adjoints.at[NT - 1, pl.ds(DEEP + (planes - RAD) * side, RAD), inner],
             adjoints.at[NT - 1, pl.ds(DEEP + planes - (planes + RAD) * side, RAD), inner],
-            halo_send.at[side, NT - 1],
-            halo_recv.at[side, NT - 1],
+            halo_send.at[0, side, NT - 1],
+            halo_recv.at[0, side, NT - 1],
             side,
         )
 
-    def first_halo(side):
-        return halo(waves, 1, 0, side, now_ref.at[pl.ds(half * side, DEEP)])
+    def first_halo(side, part):
+        return halo(waves, 1, 0, side, part, now_ref.at[pl.ds(half * side + part, RAD)])
 
     def before_halo(side):
         return remote(
@@ -193,7 +193,8 @@
 
     pl.semaphore_wait(barrier, count - 1)
     for side in range(2):
-        first_halo(side).start()
+        for part in range(0, DEEP, RAD):
+            first_halo(side, part).start()
     for side in range(2):
         before_halo(side).start()
         note_copy(side).start()
@@ -388,7 +389,8 @@
 
         def one_side(turn, carry):
             side = lax.rem(first_side + turn, 2)
-            halo(waves, step + 1, pair, 1 - side).wait_recv()
+            for part in range(0, DEEP, RAD):
+                halo(waves, step + 1, pair, 1 - side, part).wait_recv()
 
             if not begin_adjoint:
 
@@ -410,11 +412,11 @@
                         sources(NT - 1, start + i, made[i]) for i in range(RAD)
                     ]
                     store(adjoints, 1, start, first)
+                    halo(adjoints, 1, NT // 2, side, part).start()
+                else:
+                    halo(waves, step + 3, pair + 1, side, part).start()
             if begin_adjoint:
-                halo(adjoints, 1, NT // 2, side).start()
                 send_edges(NT // 2 - 2, NT - 2, side)
-            else:
-                halo(waves, step + 3, pair + 1, side).start()
             return carry
 
         lax.fori_loop(0, 2, one_side, 0)
@@ -456,7 +458,8 @@
 
         def one_side(turn, carry):
             side = lax.rem(first_side + turn, 2)
-            halo(adjoints, step, NT // 2 + pair, 1 - side).wait_recv()
+            for part in range(0, DEEP, RAD):
+                halo(adjoints, step, NT // 2 + pair, 1 - side, part).wait_recv()
             edge_copy(which, 1 - side).wait_recv()
             adjoint_beside(step, (planes + RAD) * side - RAD, which, side)
             adjoint_keep(step, (planes - RAD) * side)
@@ -466,7 +469,7 @@
             else:
                 for part in range(0, half, RAD):
                     adjoint_keep(step + 1, half * side + part)
-                halo(adjoints, step + 2, NT // 2 + pair + 1, side).start()
+                    halo(adjoints, step + 2, NT // 2 + pair + 1, side, part).start()
             return carry
 
         lax.fori_loop(0, 2, one_side, 0)
@@ -523,13 +526,15 @@
         out_ref[i] = image[period * slab + i]
 
     for side in range(2):
-        first_halo(side).wait_send()
+        for part in range(0, DEEP, RAD):
+            first_halo(side, part).wait_send()
         before_halo(side).wait_send()
         note_copy(side).wait_send()
         last_halo(side).wait_send()
         for pair in range(1, NT // 2):
-            halo(waves, 2 * pair + 1, pair, side).wait_send()
-            halo(adjoints, 2 * pair - 1, NT // 2 + pair - 1, side).wait_send()
+            for part in range(0, DEEP, RAD):
+                halo(waves, 2 * pair + 1, pair, side, part).wait_send()
+                halo(adjoints, 2 * pair - 1, NT // 2 + pair - 1, side, part).wait_send()
             edge_copy(pair - 1, side).wait_send()
 
     def sent_trace(step, carry):
@@ -599,8 +604,8 @@
             pltpu.VMEM((count, 1, span_z), jnp.float32),
             pltpu.VMEM((periods, slab, span_y, span_z), jnp.float32),
             dma((7,)),
-            dma((2, NT)),
-            dma((2, NT)),
+            dma((2, 2, NT)),
+            dma((2, 2, NT)),
             dma((2, 2)),
             dma((2, 2)),
             dma((2, NT // 2 - 1)),

time: 58.3 us -> 57.8 us (level)
  no operation moved by 1% of the time
where the time goes in v4:
time: 57.8 us; the launch traced here: 57.6 us
  Pallas kernels  55.5 us (96%)
  local copies, waits for them, and re-layouts  1.47 us (3%)
  between operations  0.66 us (1%)
    pallas_call x1, Pallas kernels, per_device(): pl.pallas_call(functools.partial(kernel, count), out_shape=jax.ShapeDtype...  55.5 us
    unnamed x1, local copies, waits for them, and re-layouts  1.47 us

profile of v4, /device:TPU:0, one launch (start us, length us, event | category | flops | bytes accessed | tf_op | source)
XLA Modules:
  0.0 57.6 jit_solution(15901667159219641202)
XLA Ops:
  0.7 55.5 %shard_map.82 = f32[4,32,128]{2,1,0:T(8,128)} custom-call(f32[64,32,128]{2,1,0:T(8,128)} %courant_ref.1, f32[16,32,128]{2,1,0:T(8,128)} %now_ref.1, f32[16,32,128]{2,1,0:T(8,128)} %before_ref.1, f32[1,8]{1,0:T(1,128)} %wavelet_ref.1, s32[1]{0:T(128)S(6)} %copy.10.source_ref, s32[1,256]{1,0:T(1,128)} %bitcast.2, s32[1,256]{1,0:T(1,128)} %bitcast.3, ...), custom_call_target="tpu_custom_call" | custom-call | tf_op jit(solution)/shard_map/pallas_call | solution.py:574
  56.1 1.5 %copy.11 = f32[4,32,128]{2,1,0:T(8,128)} copy(f32[4,32,128]{2,1,0:T(8,128)} %shard_map.82) | data formatting | bytes 131072
